TPU v7x, 32 devices: a whole 2x2x4 slice. The times are simulated.
32 devices in a mesh: groups: 2 (over y), seq: 4 (over z), eta: 2 (over x), rep: 2 (over core).
Axes of the slice: x: 2, y: 2, z: 4, core: 2. Of those that a mesh axis runs over, the one named last changes fastest.
Arguments:
- features: bfloat16 [4, 2048, 2048], P(('groups', 'eta'), 'seq', 'rep'), parts along dimension 0, may hold values from -6 to 6
- step_sizes: float32 [4, 2048, 32], P(('groups', 'eta'), 'seq', 'rep'), parts along dimension 0, may hold values from 0 to 2
- log_decay: float32 [4, 2048, 32], P(('groups', 'eta'), 'seq', 'rep'), parts along dimension 0, may hold values from -2 to 0
- state_in: bfloat16 [4, 2048, 128], P(('groups', 'eta'), 'seq'), parts along dimension 0, may hold values from -6 to 6
- state_out: bfloat16 [4, 2048, 128], P(('groups', 'eta'), 'seq'), parts along dimension 0, may hold values from -0.5 to 0.5
- skip_gain: float32 [32], P('rep'), may hold values from 0.5 to 1.5
- kernels: bfloat16 [4, 128, 128], replicated, may hold values from -0.5 to 0.5
- edge_lists: int32 [4, 4, 16, 4], P('groups', 'seq'), parts along dimension 0, may hold values from 0 to 3, as said below
- edge_counts: int32 [4, 4], P('groups', 'seq'), parts along dimension 0, may hold values from 1 to 16, as said below
- cotangent: bfloat16 [4, 2048, 2048], P(('groups', 'eta'), 'seq', 'rep'), parts along dimension 0, may hold values from -6 to 6
Outputs:
- layer_out: bfloat16 [4, 2048, 2048], P(('groups', 'eta'), 'seq', 'rep'), parts along dimension 0
- grad_features: bfloat16 [4, 2048, 2048], P(('groups', 'eta'), 'seq', 'rep'), parts along dimension 0
There are 2 independent parts, one for each index of `groups`. A program takes and returns all parts, laid end to end along the dimension named above; an argument that names none is the same for every part. Nothing has to cross between parts.
Inputs may be any that keep to these rules, and one draw needn't show every extreme that they name: `edge_lists`: rows are (source band offset 0, 1 or 2 for the band below, the same band or the band above; source block; target block; type). The used rows of a segment never name a band outside 0 to 1, and no two rows of a segment share their first three fields. `edge_counts`: every band's segments use between one and all 16 slots.
All inputs are finite; a program needn't handle non-finite values.
Results may differ from a plain program's by a relative error of at most 0.0053.
Values may be sent and summed in bfloat16 or wider, within the bound.
No kernel may reach another device: no remote copies, remote signals or barrier semaphores. Data moves between devices by JAX's collectives and lax.ppermute only.
A program may use at most 128 MiB of HBM per device.

v0:
```python
import jax
import jax.numpy as jnp
from jax import lax
from jax.sharding import PartitionSpec as P

CH = 128
BLOCK = 128


highest_prec = lax.Precision.HIGHEST


def entering_2(x, axis, combine, identity, reverse):
    peers, here = (lax.axis_size(axis), lax.axis_index(axis))
    everything = jax.tree.map(lambda part: lax.all_gather(part, axis), x)
    start = jax.tree.map(
        lambda part, zero: jnp.broadcast_to(jnp.asarray(zero, part.dtype), part.shape), x, identity
    )

    def lap(k, before):
        at = peers - 1 - k if reverse else k
        reached = at > here if reverse else at < here
        new = combine(before, jax.tree.map(lambda part: part[at], everything))
        return jax.tree.map(lambda a, b: jnp.where(reached, a, b), new, before)

    return lax.fori_loop(0, peers, lap, start)


def padded(cells, sides, width):
    for axis, dim in sides:
        count = lax.axis_size(axis)
        ends = count - 1
        head = lax.slice_in_dim(cells, 0, width, axis=dim)
        tail = lax.slice_in_dim(cells, cells.shape[dim] - width, cells.shape[dim], axis=dim)
        cells = jnp.concatenate(
            [
                lax.ppermute(tail, axis, [(i, (i + 1) % count) for i in range(ends)]),
                cells,
                lax.ppermute(head, axis, [((i + 1) % count, i) for i in range(ends)]),
            ],
            axis=dim,
        )
    return cells


def shifted(block, axis, distance):
    devices = range(lax.axis_size(axis))
    route = [(i - distance, i) for i in devices if i - distance in devices]
    return lax.ppermute(block, axis, route)


def span_parts(log_span, step_span, in_span, out_span):
    cum_log = jnp.cumsum(log_span, axis=0)
    span_len = cum_log.shape[0]
    row_ids = lax.broadcasted_iota(jnp.int32, (span_len, span_len), 0)
    col_ids = lax.broadcasted_iota(jnp.int32, (span_len, span_len), 1)
    causal = (row_ids >= col_ids)[None]
    spread = jnp.transpose(cum_log)
    differ = spread[:, :, None] - spread[:, None, :]
    decays = jnp.where(causal, jnp.exp(jnp.where(causal, differ, 0.0)), 0.0)
    scores = jnp.dot(out_span, in_span.T, preferred_element_type=jnp.float32)
    weights = (scores[None] * decays * jnp.transpose(step_span)[:, None, :]).astype(jnp.bfloat16)
    rate_terms = jnp.exp(cum_log[-1][None, :] - cum_log) * step_span
    return (cum_log, weights, rate_terms)


def span_forward(feat_span, skip_gain, cum_log, weights, rate_terms, in_span, out_span, state_now):
    inside = jnp.einsum("hij,jhp->ihp", weights, feat_span, preferred_element_type=jnp.float32)
    carried = jnp.exp(cum_log)[:, :, None] * jnp.einsum(
        "in,hpn->ihp", out_span.astype(jnp.float32), state_now, precision=highest_prec
    )
    feat_wide = feat_span.astype(jnp.float32)
    output = inside + carried + skip_gain[None, :, None] * feat_wide
    scaled = (rate_terms[:, :, None] * feat_wide).astype(jnp.bfloat16)
    state_next = jnp.exp(cum_log[-1])[:, None, None] * state_now + jnp.einsum(
        "jhp,jn->hpn", scaled, in_span, preferred_element_type=jnp.float32
    )
    return (output, state_next)


def span_backward(
    grad_span, skip_gain, cum_log, weights, rate_terms, in_span, out_span, adjoint_now
):
    through = jnp.einsum("hij,ihp->jhp", weights, grad_span, preferred_element_type=jnp.float32)
    grad_wide = grad_span.astype(jnp.float32)
    from_state = rate_terms[:, :, None] * jnp.einsum(
        "jn,hpn->jhp", in_span.astype(jnp.float32), adjoint_now, precision=highest_prec
    )
    grad_feat = through + skip_gain[None, :, None] * grad_wide + from_state
    adjoint_prev = jnp.exp(cum_log[-1])[:, None, None] * adjoint_now + jnp.einsum(
        "ihp,in->hpn",
        jnp.exp(cum_log)[:, :, None] * grad_wide,
        out_span.astype(jnp.float32),
        precision=highest_prec,
    )
    return (grad_feat, adjoint_prev)


def compose(early_part, later_part):
    decay_early, state_early = early_part
    decay_later, state_later = later_part
    return (decay_early * decay_later, decay_later[:, None, None] * state_early + state_later)


def edge_weights(edges, count, block_count, type_count):
    slot_count = edges.shape[0]
    live_slots = (jnp.arange(slot_count, dtype=jnp.int32) < count).astype(jnp.float32)
    target_hot = (edges[:, 2][:, None] == jnp.arange(block_count, dtype=jnp.int32)[None, :]).astype(
        jnp.float32
    ) * live_slots[:, None]
    kind_hot = (edges[:, 3][:, None] == jnp.arange(type_count, dtype=jnp.int32)[None, :]).astype(
        jnp.float32
    )
    return (target_hot, kind_hot)


def assemble(coefficient, kernels):
    target_blocks, source_blocks, _ = coefficient.shape
    width = kernels.shape[1]
    tiles = jnp.einsum("jsk,kab->jasb", coefficient, kernels.astype(jnp.float32))
    return tiles.reshape(target_blocks * width, source_blocks * width).astype(jnp.bfloat16)


def shards(
    features,
    step_sizes,
    log_decay,
    state_in,
    state_out,
    skip_gain,
    kernels,
    edge_lists,
    edge_counts,
    cotangent,
):
    tok_count = features.shape[1]
    feat_width = features.shape[2]
    head_count = step_sizes.shape[2]
    head_width = feat_width // head_count
    state_width = state_in.shape[2]
    span_count = tok_count // CH
    block_count = tok_count // BLOCK
    type_count = kernels.shape[0]
    feat_rows = features[0]
    step_rows = step_sizes[0]
    log_rows = log_decay[0]
    in_rows = state_in[0]
    out_rows = state_out[0]
    zero_state = jnp.zeros((head_count, head_width, state_width), jnp.float32)
    state_local = zero_state
    span_outputs = []
    span_saved = []
    for span_index in range(span_count):
        low = span_index * CH
        feat_span = feat_rows[low : low + CH].reshape(CH, head_count, head_width)
        step_span = step_rows[low : low + CH]
        log_span = log_rows[low : low + CH]
        in_span = in_rows[low : low + CH]
        out_span = out_rows[low : low + CH]
        cum_log, weights, rate_terms = span_parts(log_span, step_span, in_span, out_span)
        output, state_local = span_forward(
            feat_span, skip_gain, cum_log, weights, rate_terms, in_span, out_span, state_local
        )
        span_outputs.append(output.reshape(CH, feat_width))
        span_saved.append((cum_log, weights, rate_terms))
    partial_out = jnp.concatenate(span_outputs, axis=0)
    cum_device = jnp.cumsum(log_rows, axis=0)
    decay_device = jnp.exp(cum_device[-1])
    identity = (jnp.ones((head_count,), jnp.float32), zero_state)
    _, state_enter = entering_2((decay_device, state_local), "seq", compose, identity, False)
    entering = jnp.exp(cum_device)[:, :, None] * jnp.einsum(
        "in,hpn->ihp", out_rows.astype(jnp.float32), state_enter, precision=highest_prec
    )
    ssd_full = partial_out + entering.reshape(tok_count, feat_width)
    ssd_out = ssd_full.astype(jnp.bfloat16)
    band_now = lax.axis_index("eta")
    own_edges = edge_lists[band_now, 0]
    own_count = edge_counts[band_now, 0]
    rims = padded(ssd_out, (("eta", 0),), tok_count)
    target_hot, kind_hot = edge_weights(own_edges, own_count, block_count, type_count)
    source_index = own_edges[:, 0] * block_count + own_edges[:, 1]
    source_hot = (
        source_index[:, None] == jnp.arange(3 * block_count, dtype=jnp.int32)[None, :]
    ).astype(jnp.float32)
    coefficient = jnp.einsum("ej,es,ek->jsk", target_hot, source_hot, kind_hot)
    block_matrix = assemble(coefficient, kernels)
    message = jnp.dot(block_matrix, rims, preferred_element_type=jnp.float32)
    layer_out = (ssd_out.astype(jnp.float32) + message).astype(jnp.bfloat16)
    cot_rows = cotangent[0]
    back_terms = lax.dot_general(
        block_matrix, cot_rows, (((0,), (0,)), ((), ())), preferred_element_type=jnp.float32
    )
    back_terms = back_terms.reshape(3, tok_count, feat_width)
    from_above = shifted(back_terms[0], "eta", -1)
    from_below = shifted(back_terms[2], "eta", 1)
    grad_rows = cot_rows.astype(jnp.float32) + back_terms[1] + from_above + from_below
    ssd_grad = grad_rows.astype(jnp.bfloat16)
    adjoint_local = zero_state
    span_grads = [None] * span_count
    for span_index in reversed(range(span_count)):
        low = span_index * CH
        grad_span = ssd_grad[low : low + CH].reshape(CH, head_count, head_width)
        cum_log, weights, rate_terms = span_saved[span_index]
        grad_feat, adjoint_local = span_backward(
            grad_span,
            skip_gain,
            cum_log,
            weights,
            rate_terms,
            in_rows[low : low + CH],
            out_rows[low : low + CH],
            adjoint_local,
        )
        span_grads[span_index] = grad_feat.reshape(CH, feat_width)
    grad_part = jnp.concatenate(span_grads, axis=0)
    _, adjoint_exit = entering_2((decay_device, adjoint_local), "seq", compose, identity, True)
    rate_device = jnp.exp(cum_device[-1][None, :] - cum_device) * step_rows
    leaving = rate_device[:, :, None] * jnp.einsum(
        "jn,hpn->jhp", in_rows.astype(jnp.float32), adjoint_exit, precision=highest_prec
    )
    grad_full = grad_part + leaving.reshape(tok_count, feat_width)
    grad_features = grad_full.reshape(1, tok_count, feat_width).astype(jnp.bfloat16)
    return (layer_out.reshape(1, tok_count, feat_width), grad_features)


def solution(mesh):
    return jax.shard_map(
        shards,
        mesh=mesh,
        in_specs=(
            P(("groups", "eta"), "seq", "rep"),
            P(("groups", "eta"), "seq", "rep"),
            P(("groups", "eta"), "seq", "rep"),
            P(("groups", "eta"), "seq", None),
            P(("groups", "eta"), "seq", None),
            P("rep"),
            P(),
            P("groups", "seq", None, None),
            P("groups", "seq"),
            P(("groups", "eta"), "seq", "rep"),
        ),
        out_specs=(P(("groups", "eta"), "seq", "rep"), P(("groups", "eta"), "seq", "rep")),
        check_vma=False,
    )
```

profile of v0, /device:TPU:0, one launch (start us, length us, event | category | flops | bytes accessed | tf_op | source)
XLA Modules:
  0.0 169.8 jit_solution(7260961802961636623)
XLA Ops:
  10.3 1.3 fusion.145
  19.9 2.4 %convolution_convert_fusion = bf16[4,12,128,128]{3,1,2,0:T(8,128)(2,1)} fusion(bf16[4,128,128]{2,1,0:T(8,128)(2,1)S(1)} %copy-done.33, s32[16]{0:T(128)S(1)} %get-tuple-element.329, f32[16,4]{0,1:T(4,128)S(1)} %fusion.126, f32[16,4]{0,1:T(4,128)S(1)} %fusion.125), kind=kOutput, calls=%fused_computation.23 | convolution fusion | flops 7084480 | bytes 1704512 | tf_op jit(solution)/shard_map/jsk,kab->jasb/dot_general | solution.py:120
  22.3 3.8 %fusion.14 = f32[1536,1024]{0,1:T(8,128)S(1)} fusion(bf16[64,8,12,128]{3,2,1,0:T(8,128)(2,1)} %bitcast.395, bf16[1,512,1024]{2,1,0:T(8,128)(2,1)} %param.23), kind=kOutput, calls=%fused_computation.25 | convolution fusion | flops 1610612736 | bytes 8912896 | tf_op jit(solution)/shard_map/dot_general | solution.py:190
  26.2 2.4 %fusion.143 = (f32[512,1024]{0,1:T(8,128)}, f32[512,1024]{0,1:T(8,128)}) fusion(f32[1536,1024]{0,1:T(8,128)S(1)} %fusion.14), kind=kLoop, calls=%fused_computation.212 | loop fusion | bytes 8388608 | tf_op jit(solution)/shard_map/slice | solution.py:194
  28.6 1.6 copy-done.1
  30.2 6.3 %collective-permute-start.3 = (f32[512,1024]{0,1:T(8,128)}, f32[512,1024]{0,1:T(8,128)}, u32[]{:S(2)}, u32[]{:S(2)}) collective-permute-start(f32[512,1024]{0,1:T(8,128)} %get-tuple-element.289), channel_id=1, source_target_pairs={{0,2},{1,3},{4,6},{5,7},{8,10},{9,11},{12,14},{13,15},{16,18},{17,... | collective-permute-start | bytes 6291464 | tf_op jit(solution)/shard_map/ppermute | solution.py:49
  36.5 1.3 collective-permute-start.2
  38.7 1.4 convolution_bitcast_fusion.9
  40.1 1.4 convolution_bitcast_fusion.11
  41.5 1.4 convolution_bitcast_fusion.13
  42.9 1.4 convolution_bitcast_fusion.15
  44.9 2.3 %copy.153 = bf16[1,512,1024]{1,2,0:T(8,128)(2,1)} copy(bf16[1,512,1024]{2,1,0:T(8,128)(2,1)} %param.23) | data formatting | bytes 2097152 | tf_op args[9]
  47.2 3.1 %reduce-window.6 = f32[16,4,128]{2,0,1:T(8,128)} reduce-window(f32[16,4,128]{2,0,1:T(8,128)} %copy_bitcast_fusion, f32[]{:T(128)} %constant.85.clone.1), window={size=1x1x128 pad=0_0x0_0x127_0}, to_apply=%region_4.5 | reduce-window | flops 1040384 | bytes 65540 | tf_op jit(solution)/shard_map/reduce-window
  50.3 1.5 copy.141
  51.8 1.5 copy.133
  53.3 1.5 copy.125
  54.8 2.3 %fusion.36 = f32[128,16,64]{0,2,1:T(8,128)} fusion(f32[128,16,64]{0,2,1:T(8,128)} %convolution_bitcast_fusion.9, f32[16,64,128]{2,1,0:T(8,128)S(1)} %convolution_add_fusion.1, bf16[128,16,64]{0,2,1:T(8,128)(2,1)S(1)} %bitcast.386, f32[128,16]{0,1:T(8,128)} %copy.141, f32[16]{0:T(128)S(1)} %copy-done.65, bf16[1,512,128]{2,1,0:T(8,128)(2,1)S(1)} %copy-done.9), kind=kOutput, calls=%fused_computation.59 | convolution fusion | flops 201981952 | bytes 1876480 | tf_op jit(solution)/shard_map/in,hpn->ihp/dot_general | solution.py:69
  57.2 2.0 %fusion.33 = f32[128,16,64]{0,2,1:T(8,128)} fusion(f32[128,16,64]{0,2,1:T(8,128)S(1)} %copy-done.28, f32[16,64,128]{2,1,0:T(8,128)S(1)} %convolution_add_fusion.2, bf16[128,16,64]{0,2,1:T(8,128)(2,1)S(1)} %bitcast.388, f32[128,16]{0,1:T(8,128)} %copy.133, f32[16]{0:T(128)S(1)} %copy-done.65, bf16[1,512,128]{2,1,0:T(8,128)(2,1)S(1)} %copy-done.9), kind=kOutput, calls=%fused_computation.56 | convolution fusion | flops 201981952 | bytes 1876480 | tf_op jit(solution)/shard_map/in,hpn->ihp/dot_general | solution.py:69
  59.2 1.2 fusion.30
  62.6 2.1 %copy.144 = f32[128,1024]{1,0:T(8,128)} copy(f32[128,1024]{0,1:T(8,128)} %bitcast.400) | data formatting | bytes 1048576 | tf_op jit(solution)/shard_map/reshape | solution.py:164
  65.7 1.4 fusion.27
  68.4 11.4 %all-gather.2 = f32[4,1,16]{2,1,0:T(1,128)} all-gather(f32[1,1,16]{2,1,0:T(1,128)S(1)} %bitcast.417), channel_id=1, replica_groups=mesh['groups'=2,'seq'=4,'eta'=2,'rep'=2] {'seq'}, dimensions={0}, use_global_device_ids=true | all-gather | bytes 320 | tf_op jit(solution)/shard_map/all_gather | solution.py:15
  80.5 2.0 %fusion.40 = f32[128,16,64]{0,2,1:T(8,128)} fusion(f32[128,16]{0,1:T(8,128)S(1)} %copy-done.42, bf16[1,512,128]{2,1,0:T(8,128)(2,1)} %param.17), kind=kOutput, calls=%fused_computation.63 | convolution fusion | flops 201457664 | bytes 565248 | tf_op jit(solution)/shard_map/jn,hpn->jhp/dot_general | solution.py:86
  82.5 3.4 %collective-permute-done.2 = f32[512,1024]{0,1:T(8,128)} collective-permute-done((f32[512,1024]{0,1:T(8,128)}, f32[512,1024]{0,1:T(8,128)}, u32[]{:S(2)}, u32[]{:S(2)}) %collective-permute-start.2) | collective-permute-done | bytes 2097184 | tf_op jit(solution)/shard_map/ppermute | solution.py:49
  85.8 3.8 %fusion.10 = bf16[512,1024]{0,1:T(8,128)(2,1)S(1)} fusion(f32[512,1024]{0,1:T(8,128)} %collective-permute-done.3, f32[512,1024]{0,1:T(8,128)} %collective-permute-done.2, f32[1536,1024]{0,1:T(8,128)} %copy-done.1, bf16[1,512,1024]{1,2,0:T(8,128)(2,1)S(1)} %copy-done.6), kind=kLoop, calls=%fused_computation.15 | loop fusion | flops 2621440 | bytes 8388608 | tf_op jit(solution)/shard_map/convert_element_type | solution.py:197
  91.0 1.9 %fusion.39 = f32[128,16,64]{0,2,1:T(8,128)} fusion(f32[16,64,128]{2,1,0:T(8,128)S(1)} %convolution_add_fusion.7, f32[128,16]{0,1:T(8,128)S(1)} %copy-done.40, bf16[1,512,128]{2,1,0:T(8,128)(2,1)} %param.17), kind=kOutput, calls=%fused_computation.62 | convolution fusion | flops 201457664 | bytes 1089536 | tf_op jit(solution)/shard_map/jn,hpn->jhp/dot_general | solution.py:86
  96.2 1.2 convolution_add_fusion.4
  97.5 2.5 %fusion.48 = f32[128,16,64]{0,2,1:T(8,128)} fusion(f32[128,16,64]{0,2,1:T(8,128)} %fusion.40, bf16[128,16,64]{0,2,1:T(8,128)(2,1)S(1)} %bitcast.416, f32[16,128]{1,0:T(8,128)} %get-tuple-element.319, f32[16,128]{1,0:T(8,128)} %copy-done.64, f32[128,128]{1,0:T(8,128)} %copy-done.52, pred[128,128]{1,0:T(8,128)(4,1)} %copy-done.53, f32[16]{0:T(128)S(1)} %copy-done.66), kind=kOutput, calls=%fused_computation.75 | convolution fusion | flops 35651584 | bytes 1409088 | tf_op jit(solution)/shard_map/hij,ihp->jhp/dot_general | solution.py:84
  100.0 7.5 %while.30 = (s32[]{:T(128)}, f32[16,64,128]{2,1,0:T(8,128)S(1)}, s32[]{:T(128)}, f32[4,16]{1,0:T(4,128)}, f32[4,16,64,128]{3,2,1,0:T(8,128)}, /*index=5*/s32[]{:T(128)}, s32[]{:T(128)}) while((s32[]{:T(128)}, f32[16,64,128]{2,1,0:T(8,128)S(1)}, s32[]{:T(128)}, f32[4,16]{1,0:T(4,128)}, f32[4,16,64,128]{3,2,1,0:T(8,128)}, ...), condition=%wide.region_7.8_spmd.clone, body=%wide.region_6.7_spmd.clone.sunk | while | flops 524292 | bytes 1573169 | solution.py:26
  100.7 1.2 fusion.177
  102.6 1.2 fusion.177
  104.4 1.2 fusion.177
  106.3 1.2 fusion.177
  107.5 2.3 %bitcast_multiply_fusion.1 = f32[512,16,64]{0,2,1:T(8,128)} fusion(f32[16,64,128]{2,1,0:T(8,128)S(1)} %get-tuple-element.228, f32[512,16]{0,1:T(8,128)S(1)} %copy-done.32, bf16[1,512,128]{2,1,0:T(8,128)(2,1)S(1)} %copy-done.9), kind=kOutput, calls=%fused_computation.21 | convolution fusion | flops 805830656 | bytes 2785280 | tf_op jit(solution)/shard_map/in,hpn->ihp/dot_general | solution.py:171
  109.9 2.0 %copy.150 = f32[512,1024]{1,0:T(8,128)S(1)} copy(f32[512,1024]{0,1:T(8,128)} %bitcast.379) | data formatting | bytes 4194304 | tf_op jit(solution)/shard_map/reshape | solution.py:174
  111.9 2.8 %fusion.11 = bf16[512,1024]{1,0:T(8,128)(2,1)} fusion(f32[512,1024]{1,0:T(8,128)S(1)} %copy.150, f32[128,1024]{1,0:T(8,128)S(1)} %copy-done.10, f32[128,1024]{1,0:T(8,128)} %copy.145, f32[128,1024]{1,0:T(8,128)} %copy.144, f32[128,1024]{1,0:T(8,128)} %copy.143), kind=kLoop, calls=%fused_computation.17 | loop fusion | flops 2621440 | bytes 5242880 | tf_op jit(solution)/shard_map/convert_element_type | solution.py:175
  114.7 1.4 collective-permute-start.1
  116.1 6.5 %collective-permute-start = (bf16[512,1024]{1,0:T(8,128)(2,1)}, bf16[512,1024]{1,0:T(8,128)(2,1)}, u32[]{:S(2)}, u32[]{:S(2)}) collective-permute-start(bf16[512,1024]{1,0:T(8,128)(2,1)} %fusion.11), channel_id=1, source_target_pairs={{0,2},{1,3},{4,6},{5,7},{8,10},{9,11},{12,14},{13,15},{16,18},{17,... | collective-permute-start | bytes 3145736 | tf_op jit(solution)/shard_map/ppermute | solution.py:37
  124.2 1.8 %fusion.44 = f32[128,16,64]{0,2,1:T(8,128)S(1)} fusion(f32[128,16,64]{0,2,1:T(8,128)S(1)} %fusion.38, bf16[128,16,64]{0,2,1:T(8,128)(2,1)} %bitcast.414, f32[16,128]{1,0:T(8,128)} %get-tuple-element.317, f32[16,128]{1,0:T(8,128)} %copy-done.61, f32[128,128]{1,0:T(8,128)} %copy-done.49, pred[128,128]{1,0:T(8,128)(4,1)} %copy-done.53, f32[16]{0:T(128)S(1)} %copy-done.66), kind=kOutput, calls=%fused_computation.71 | convolution fusion | flops 35651584 | bytes 1409088 | tf_op jit(solution)/shard_map/hij,ihp->jhp/dot_general | solution.py:84
  127.4 1.4 fusion.42
  129.8 11.1 %collective-permute-done.1 = bf16[512,1024]{1,0:T(8,128)(2,1)} collective-permute-done((bf16[512,1024]{1,0:T(8,128)(2,1)}, bf16[512,1024]{1,0:T(8,128)(2,1)}, u32[]{:S(2)}, u32[]{:S(2)}) %collective-permute-start.1) | collective-permute-done | bytes 1048608 | tf_op jit(solution)/shard_map/ppermute | solution.py:39
  140.9 2.2 %collective-permute-done = bf16[512,1024]{1,0:T(8,128)(2,1)} collective-permute-done((bf16[512,1024]{1,0:T(8,128)(2,1)}, bf16[512,1024]{1,0:T(8,128)(2,1)}, u32[]{:S(2)}, u32[]{:S(2)}) %collective-permute-start) | collective-permute-done | bytes 1048608 | tf_op jit(solution)/shard_map/ppermute | solution.py:37
  143.0 5.7 %fusion.20 = bf16[1,512,1024]{2,1,0:T(8,128)(2,1)} fusion(bf16[512,1024]{1,0:T(8,128)(2,1)} %collective-permute-done.1, bf16[512,1024]{1,0:T(8,128)(2,1)} %fusion.11, bf16[512,1024]{1,0:T(8,128)(2,1)} %collective-permute-done, bf16[64,8,12,128]{3,2,1,0:T(8,128)(2,1)} %bitcast.396), kind=kOutput, calls=%fused_computation.27 | convolution fusion | flops 1621622784 | bytes 5767168 | tf_op jit(solution)/shard_map/dot_general | solution.py:187
  148.7 7.5 %while.31 = (s32[]{:T(128)}, f32[16,64,128]{2,1,0:T(8,128)S(1)}, s32[]{:T(128)}, f32[4,16]{1,0:T(4,128)}, f32[4,16,64,128]{3,2,1,0:T(8,128)}, /*index=5*/s32[]{:T(128)}, s32[]{:T(128)}, s32[]{:T(128)}, s32[]{:T(128)}) while((s32[]{:T(128)}, f32[16,64,128]{2,1,0:T(8,128)S(1)}, s32[]{:T(128)}, f32[4,16]{1,0:T(4,128)}, ...), condition=%wide.region_9.10_spmd.clone, body=%wide.region_8.9_spmd.clone.sunk | while | flops 524296 | bytes 1573231 | solution.py:26
  149.4 1.2 fusion.178
  156.2 2.3 %bitcast_multiply_fusion = f32[512,16,64]{0,2,1:T(8,128)} fusion(f32[16,64,128]{2,1,0:T(8,128)S(1)} %get-tuple-element.229, f32[512,16]{0,1:T(8,128)S(1)} %copy-done.31, bf16[1,512,128]{2,1,0:T(8,128)(2,1)S(1)} %copy-done.12), kind=kOutput, calls=%fused_computation.20 | convolution fusion | flops 805830656 | bytes 2785280 | tf_op jit(solution)/shard_map/jn,hpn->jhp/dot_general | solution.py:218
  158.5 1.9 %copy.158 = f32[1,512,1024]{2,1,0:T(8,128)S(1)} copy(f32[1,512,1024]{1,2,0:T(8,128)} %bitcast.380) | data formatting | bytes 4194304 | tf_op jit(solution)/shard_map/reshape | solution.py:221
  160.5 2.5 %fusion.12 = bf16[1,512,1024]{2,1,0:T(8,128)(2,1)} fusion(f32[1,512,1024]{2,1,0:T(8,128)S(1)} %copy.158, f32[1,128,1024]{2,1,0:T(8,128)S(1)} %copy.157, f32[1,128,1024]{2,1,0:T(8,128)S(1)} %copy.156, f32[1,128,1024]{2,1,0:T(8,128)} %copy.155, f32[1,128,1024]{2,1,0:T(8,128)} %copy.154), kind=kLoop, calls=%fused_computation.19 | loop fusion | flops 2621440 | bytes 5242880 | tf_op jit(solution)/shard_map/convert_element_type | solution.py:222
  (249 shorter events, 35.2 us)
Async XLA Ops:
  7.2 11.4 %copy-start = (s32[2,1,16,4]{2,3,1,0:T(4,128)S(1)}, s32[2,1,16,4]{2,3,1,0:T(4,128)}, u32[]{:S(2)}) copy-start(s32[2,1,16,4]{2,3,1,0:T(4,128)} %param.21) | copy-start | bytes 1540
  7.2 4.5 %copy-start.35 = (f32[1,512,16]{1,2,0:T(8,128)S(1)}, f32[1,512,16]{1,2,0:T(8,128)}, u32[]{:S(2)}) copy-start(f32[1,512,16]{1,2,0:T(8,128)} %param.15) | copy-start | bytes 98308
  7.2 92.8 %all-gather.6.cloned.1.call-start = ((), (), s32[]{:S(2)}) async-start(), calls=%async_computation | async-start | bytes 2621440 | tf_op jit(solution)/shard_map/all_gather | solution.py:15
  8.3 7.2 %copy-start.15 = (f32[128,16]{1,0:T(8,128)}, f32[128,16]{1,0:T(8,128)S(1)}, u32[]{:S(2)}) copy-start(f32[128,16]{1,0:T(8,128)S(1)} %reduce_window_sum.44) | copy-start | bytes 24580
  9.1 5.3 %copy-start.17 = (f32[128,16]{1,0:T(8,128)}, f32[128,16]{1,0:T(8,128)S(1)}, u32[]{:S(2)}) copy-start(f32[128,16]{1,0:T(8,128)S(1)} %reduce_window_sum.45) | copy-start | bytes 24580
  9.1 7.9 %copy-start.67 = (f32[16]{0:T(128)}, f32[16]{0:T(128)S(1)}, u32[]{:S(2)}) copy-start(f32[16]{0:T(128)S(1)} %fusion.139) | copy-start | bytes 196
  9.4 4.0 %copy-start.19 = (f32[128,16]{1,0:T(8,128)}, f32[128,16]{1,0:T(8,128)S(1)}, u32[]{:S(2)}) copy-start(f32[128,16]{1,0:T(8,128)S(1)} %reduce_window_sum.46) | copy-start | bytes 24580
  9.5 7.8 %copy-start.69 = (f32[16]{0:T(128)}, f32[16]{0:T(128)S(1)}, u32[]{:S(2)}) copy-start(f32[16]{0:T(128)S(1)} %fusion.140) | copy-start | bytes 196
  9.7 3.7 %copy-start.21 = (f32[128,16]{1,0:T(8,128)}, f32[128,16]{1,0:T(8,128)S(1)}, u32[]{:S(2)}) copy-start(f32[128,16]{1,0:T(8,128)S(1)} %reduce_window_sum.47) | copy-start | bytes 24580
  14.4 27.1 %copy-start.7 = (bf16[1,128,1024]{1,2,0:T(8,128)(2,1)}, bf16[1,128,1024]{1,2,0:T(8,128)(2,1)S(1)}, u32[]{:S(2)}) copy-start(bf16[1,128,1024]{1,2,0:T(8,128)(2,1)S(1)} %copy.164) | copy-start | bytes 786436
  18.5 130.2 %all-gather.8.cloned.1.call-start = ((), (), s32[]{:S(2)}) async-start(), calls=%async_computation.1 | async-start | bytes 2621440 | tf_op jit(solution)/shard_map/all_gather | solution.py:15
  26.1 4.1 %copy-start.1 = (f32[1536,1024]{0,1:T(8,128)}, f32[1536,1024]{0,1:T(8,128)S(1)}, u32[]{:S(2)}) copy-start(f32[1536,1024]{0,1:T(8,128)S(1)} %fusion.14) | copy-start | bytes 18874372
  26.1 11.7 %copy-start.9 = (bf16[1,512,128]{2,1,0:T(8,128)(2,1)S(1)}, bf16[1,512,128]{2,1,0:T(8,128)(2,1)}, u32[]{:S(2)}) copy-start(bf16[1,512,128]{2,1,0:T(8,128)(2,1)} %param.18) | copy-start | bytes 393220
  26.1 12.3 %copy-start.22 = (f32[128,16]{1,0:T(8,128)S(1)}, f32[128,16]{1,0:T(8,128)}, u32[]{:S(2)}) copy-start(f32[128,16]{1,0:T(8,128)} %copy-done.21) | copy-start | bytes 24580
  26.1 12.4 %copy-start.20 = (f32[128,16]{1,0:T(8,128)S(1)}, f32[128,16]{1,0:T(8,128)}, u32[]{:S(2)}) copy-start(f32[128,16]{1,0:T(8,128)} %copy-done.19) | copy-start | bytes 24580
  26.1 12.5 %copy-start.18 = (f32[128,16]{1,0:T(8,128)S(1)}, f32[128,16]{1,0:T(8,128)}, u32[]{:S(2)}) copy-start(f32[128,16]{1,0:T(8,128)} %copy-done.17) | copy-start | bytes 24580
  26.1 12.5 %copy-start.16 = (f32[128,16]{1,0:T(8,128)S(1)}, f32[128,16]{1,0:T(8,128)}, u32[]{:S(2)}) copy-start(f32[128,16]{1,0:T(8,128)} %copy-done.15) | copy-start | bytes 24580
  26.1 12.6 %copy-start.59 = (f32[16,128]{1,0:T(8,128)S(1)}, f32[16,128]{1,0:T(8,128)}, u32[]{:S(2)}) copy-start(f32[16,128]{1,0:T(8,128)} %get-tuple-element.319) | copy-start | bytes 24580
  30.2 9.9 %copy-start.57 = (f32[16,128]{1,0:T(8,128)S(1)}, f32[16,128]{1,0:T(8,128)}, u32[]{:S(2)}) copy-start(f32[16,128]{1,0:T(8,128)} %get-tuple-element.318) | copy-start | bytes 24580
  30.2 52.3 %collective-permute-start.3 = (f32[512,1024]{0,1:T(8,128)}, f32[512,1024]{0,1:T(8,128)}, u32[]{:S(2)}, u32[]{:S(2)}) collective-permute-start(f32[512,1024]{0,1:T(8,128)} %get-tuple-element.289), channel_id=1, source_target_pairs={{0,2},{1,3},{4,6},{5,7},{8,10},{9,11},{12,14},{13,15},{16,18},{17,... | collective-permute-start | bytes 6291464 | tf_op jit(solution)/shard_map/ppermute | solution.py:49
  36.5 49.3 %collective-permute-start.2 = (f32[512,1024]{0,1:T(8,128)}, f32[512,1024]{0,1:T(8,128)}, u32[]{:S(2)}, u32[]{:S(2)}) collective-permute-start(f32[512,1024]{0,1:T(8,128)} %get-tuple-element.288), channel_id=1, source_target_pairs={{2,0},{3,1},{6,4},{7,5},{10,8},{11,9},{14,12},{15,13},{18,16},{19,... | collective-permute-start | bytes 6291464 | tf_op jit(solution)/shard_map/ppermute | solution.py:49
  37.8 5.1 %copy-start.53 = (pred[128,128]{1,0:T(8,128)(4,1)}, pred[128,128]{1,0:T(8,128)(4,1)S(1)}, u32[]{:S(2)}) copy-start(pred[128,128]{1,0:T(8,128)(4,1)S(1)} %iota_compare_fusion) | copy-start | bytes 49156
  37.9 3.5 %copy-start.52 = (f32[128,128]{1,0:T(8,128)}, f32[128,128]{1,0:T(8,128)S(1)}, u32[]{:S(2)}) copy-start(f32[128,128]{1,0:T(8,128)S(1)} %fusion.68) | copy-start | bytes 196612
  38.4 4.5 %copy-start.48 = (f32[128,128]{1,0:T(8,128)}, f32[128,128]{1,0:T(8,128)S(1)}, u32[]{:S(2)}) copy-start(f32[128,128]{1,0:T(8,128)S(1)} %fusion.87) | copy-start | bytes 196612
  38.7 4.2 %copy-start.60 = (f32[16,128]{1,0:T(8,128)}, f32[16,128]{1,0:T(8,128)S(1)}, u32[]{:S(2)}) copy-start(f32[16,128]{1,0:T(8,128)S(1)} %copy.113) | copy-start | bytes 24580
  42.9 11.9 %copy-start.65 = (f32[16]{0:T(128)S(1)}, f32[16]{0:T(128)}, u32[]{:S(2)}) copy-start(f32[16]{0:T(128)} %param.19) | copy-start | bytes 196
  54.8 4.3 %copy-start.8 = (bf16[1,128,1024]{1,2,0:T(8,128)(2,1)S(1)}, bf16[1,128,1024]{1,2,0:T(8,128)(2,1)}, u32[]{:S(2)}) copy-start(bf16[1,128,1024]{1,2,0:T(8,128)(2,1)} %copy-done.7) | copy-start | bytes 786436
  54.8 4.3 %copy-start.27 = (f32[128,16,64]{0,2,1:T(8,128)S(1)}, f32[128,16,64]{0,2,1:T(8,128)}, u32[]{:S(2)}) copy-start(f32[128,16,64]{0,2,1:T(8,128)} %convolution_bitcast_fusion.13) | copy-start | bytes 1572868
  54.8 4.3 %copy-start.45 = (f32[128,16]{0,1:T(8,128)S(1)}, f32[128,16]{0,1:T(8,128)}, u32[]{:S(2)}) copy-start(f32[128,16]{0,1:T(8,128)} %copy.125) | copy-start | bytes 24580
  61.6 6.5 %copy-start.26 = (f32[16,4,128]{2,0,1:T(8,128)S(1)}, f32[16,4,128]{2,0,1:T(8,128)}, u32[]{:S(2)}) copy-start(f32[16,4,128]{2,0,1:T(8,128)} %reduce-window.6) | copy-start | bytes 98308
  61.6 18.2 %copy-start.36 = (f32[1,512,16]{1,2,0:T(8,128)S(1)}, f32[1,512,16]{1,2,0:T(8,128)}, u32[]{:S(2)}) copy-start(f32[1,512,16]{1,2,0:T(8,128)} %param.15) | copy-start | bytes 98308
  62.6 17.9 %copy-start.42 = (f32[128,16]{0,1:T(8,128)S(1)}, f32[128,16]{0,1:T(8,128)}, u32[]{:S(2)}) copy-start(f32[128,16]{0,1:T(8,128)} %copy-done.41) | copy-start | bytes 24580
  62.6 23.2 %copy-start.6 = (bf16[1,512,1024]{1,2,0:T(8,128)(2,1)S(1)}, bf16[1,512,1024]{1,2,0:T(8,128)(2,1)}, u32[]{:S(2)}) copy-start(bf16[1,512,1024]{1,2,0:T(8,128)(2,1)} %copy.153) | copy-start | bytes 3145732
  65.7 20.2 %copy-start.47 = (f32[128,16]{0,1:T(8,128)}, f32[128,16]{0,1:T(8,128)S(1)}, u32[]{:S(2)}) copy-start(f32[128,16]{0,1:T(8,128)S(1)} %copy.118) | copy-start | bytes 24580
  82.4 7.2 %copy-start.43 = (f32[128,16]{0,1:T(8,128)S(1)}, f32[128,16]{0,1:T(8,128)}, u32[]{:S(2)}) copy-start(f32[128,16]{0,1:T(8,128)} %copy.141) | copy-start | bytes 24580
  82.5 7.2 %copy-start.44 = (f32[128,16]{0,1:T(8,128)S(1)}, f32[128,16]{0,1:T(8,128)}, u32[]{:S(2)}) copy-start(f32[128,16]{0,1:T(8,128)} %copy.133) | copy-start | bytes 24580
  82.5 7.2 %copy-start.46 = (f32[128,16]{0,1:T(8,128)S(1)}, f32[128,16]{0,1:T(8,128)}, u32[]{:S(2)}) copy-start(f32[128,16]{0,1:T(8,128)} %copy.125) | copy-start | bytes 24580
  100.0 7.5 %copy-start.32 = (f32[512,16]{0,1:T(8,128)S(1)}, f32[512,16]{0,1:T(8,128)}, u32[]{:S(2)}) copy-start(f32[512,16]{0,1:T(8,128)} %get-tuple-element.315) | copy-start | bytes 98308
  111.9 10.8 %copy-start.23 = (f32[128,16,64]{0,2,1:T(8,128)S(1)}, f32[128,16,64]{0,2,1:T(8,128)}, u32[]{:S(2)}) copy-start(f32[128,16,64]{0,2,1:T(8,128)} %fusion.39) | copy-start | bytes 1572868
  111.9 10.8 %copy-start.30 = (bf16[128,1024]{0,1:T(8,128)(2,1)S(1)}, bf16[128,1024]{0,1:T(8,128)(2,1)}, u32[]{:S(2)}) copy-start(bf16[128,1024]{0,1:T(8,128)(2,1)} %get-tuple-element.292) | copy-start | bytes 786436
  111.9 10.8 %copy-start.51 = (f32[128,128]{1,0:T(8,128)S(1)}, f32[128,128]{1,0:T(8,128)}, u32[]{:S(2)}) copy-start(f32[128,128]{1,0:T(8,128)} %copy-done.50) | copy-start | bytes 196612
  111.9 10.8 %copy-start.54 = (pred[128,128]{1,0:T(8,128)(4,1)S(1)}, pred[128,128]{1,0:T(8,128)(4,1)}, u32[]{:S(2)}) copy-start(pred[128,128]{1,0:T(8,128)(4,1)} %copy-done.53) | copy-start | bytes 49156
  111.9 10.8 %copy-start.58 = (f32[16,128]{1,0:T(8,128)S(1)}, f32[16,128]{1,0:T(8,128)}, u32[]{:S(2)}) copy-start(f32[16,128]{1,0:T(8,128)} %get-tuple-element.318) | copy-start | bytes 24580
  111.9 10.8 %copy-start.63 = (f32[16,128]{1,0:T(8,128)S(1)}, f32[16,128]{1,0:T(8,128)}, u32[]{:S(2)}) copy-start(f32[16,128]{1,0:T(8,128)} %copy-done.62) | copy-start | bytes 24580
  114.7 8.6 %copy-start.24 = (f32[128,16,64]{0,2,1:T(8,128)S(1)}, f32[128,16,64]{0,2,1:T(8,128)}, u32[]{:S(2)}) copy-start(f32[128,16,64]{0,2,1:T(8,128)} %fusion.48) | copy-start | bytes 1572868
  114.7 26.1 %collective-permute-start.1 = (bf16[512,1024]{1,0:T(8,128)(2,1)}, bf16[512,1024]{1,0:T(8,128)(2,1)}, u32[]{:S(2)}, u32[]{:S(2)}) collective-permute-start(bf16[512,1024]{1,0:T(8,128)(2,1)} %fusion.11), channel_id=1, source_target_pairs={{2,0},{3,1},{6,4},{7,5},{10,8},{11,9},{14,12},{15,13},{18,16},{19,... | collective-permute-start | bytes 3145736 | tf_op jit(solution)/shard_map/ppermute | solution.py:39
  116.1 26.9 %collective-permute-start = (bf16[512,1024]{1,0:T(8,128)(2,1)}, bf16[512,1024]{1,0:T(8,128)(2,1)}, u32[]{:S(2)}, u32[]{:S(2)}) collective-permute-start(bf16[512,1024]{1,0:T(8,128)(2,1)} %fusion.11), channel_id=1, source_target_pairs={{0,2},{1,3},{4,6},{5,7},{8,10},{9,11},{12,14},{13,15},{16,18},{17,... | collective-permute-start | bytes 3145736 | tf_op jit(solution)/shard_map/ppermute | solution.py:37
  148.7 7.5 %copy-start.31 = (f32[512,16]{0,1:T(8,128)S(1)}, f32[512,16]{0,1:T(8,128)}, u32[]{:S(2)}) copy-start(f32[512,16]{0,1:T(8,128)} %get-tuple-element.314) | copy-start | bytes 98308
  (33 other events, 76.4 us)
Sparse Core Ops, SparseCore 0:
  18.6 48.3 all-gather.5
  97.6 45.9 all-gather.7
where the time goes:
time: 172 us; the launch traced here: 170 us
  matrix products  44.4 us (26%)
  local copies, waits for them, and re-layouts  38.2 us (22%)
  other arithmetic  28.6 us (17%)
  waiting for transfers between devices  16.7 us (10%)
  starting transfers between devices  15.6 us (9%)
  between operations  15 us (9%)
  blocking collectives  11.4 us (7%)
    all_gather x1, blocking collectives, entering_2(): everything = jax.tree.map(lambda part: lax.all_gather(part, axis), x)  11.4 us
    ppermute x1, waiting for transfers between devices, padded(): lax.ppermute(head, axis, [((i + 1) % count, i) for i in range(ends)])  11.1 us
    select_n x8, other arithmetic, lap(): return jax.tree.map(lambda a, b: jnp.where(reached, a, b), new, before)  9.41 us
    ppermute x2, starting transfers between devices, shifted(): return lax.ppermute(block, axis, route)  7.56 us
    unnamed x159, local copies, waits for them, and re-layouts  7.35 us
    dot_general x4, matrix products, span_forward(): jnp.einsum('in,hpn->ihp', out_span.astype(jnp.float32), state_now, precis...  6.97 us
    ppermute x1, starting transfers between devices, padded(): lax.ppermute(tail, axis, [(i, (i + 1) % count) for i in range(ends)])  6.51 us
    dot_general x4, matrix products, span_backward(): jnp.einsum('hij,ihp->jhp', weights, grad_span, preferred_element_type=jnp...  6.26 us
  transfers between devices with their start and end apart: 6, of which 3 were waited for; matrix products, arithmetic and copies ran while one was open for 49% of the time, Pallas kernels for 0%

commit v1 on v0

v1 whole, which is shorter than its diff:
```python
import jax
import jax.numpy as jnp
from jax import lax
from jax.experimental import pallas as pl
from jax.experimental.pallas import tpu as pltpu
from jax.sharding import PartitionSpec as P

CH = 128
BLOCK = 128
PAD = 16
GROUPS = 2

F32 = jnp.float32
BF16 = jnp.bfloat16


def dot(a, b):
    return jnp.dot(a, b, preferred_element_type=F32)


def dot_rows(a, b):
    return lax.dot_general(a, b, (((0,), (0,)), ((), ())), preferred_element_type=F32)


def pieces(x, count):
    out = []
    for _ in range(count):
        part = x.astype(BF16)
        out.append(part)
        x = x - part.astype(F32)
    return out


def spread_matrix(heads, width, first, head_width):
    row = lax.broadcasted_iota(jnp.int32, (heads, width), 0)
    col = lax.broadcasted_iota(jnp.int32, (heads, width), 1)
    low = (row - first) * head_width
    return ((col >= low) & (col < low + head_width)).astype(F32).astype(BF16)


def spread(x, matrix):
    high, low = pieces(x, 2)
    return dot(high, matrix) + dot(low, matrix)


def run(kernel, outs, args, in_specs=None, out_specs=None, aliases=None, us=1.0, name=None, **kw):
    vmem = pl.BlockSpec(memory_space=pltpu.VMEM)
    return pl.pallas_call(
        kernel,
        out_shape=outs,
        in_specs=in_specs or [vmem] * len(args),
        out_specs=out_specs or jax.tree.map(lambda _: vmem, outs),
        input_output_aliases=aliases or {},
        cost_estimate=pl.CostEstimate(
            flops=0, bytes_accessed=int(us * 3.0e6), transcendentals=0
        ),
        name=name,
        **kw,
    )(*args)


def shape(dims, kind):
    return jax.ShapeDtypeStruct(dims, kind)


class Plan:
    def __init__(self, tok, width, heads, state):
        self.tok, self.width, self.heads, self.state = tok, width, heads, state
        self.head_width = width // heads
        self.spans = tok // CH
        self.groups = GROUPS
        self.part = width // GROUPS
        self.group_heads = heads // GROUPS
        self.blocks = tok // BLOCK


def pack_tail(total, part):
    tail = jnp.concatenate([p.astype(F32) for p in pieces(total, 3)], axis=0)
    return jnp.concatenate([tail, jnp.zeros((PAD - 3, part), F32)], axis=0).astype(BF16)


def unpack_tail(ref, rows):
    tail = ref[rows : rows + PAD, :].astype(F32)
    return tail[0:1] + tail[1:2] + tail[2:3]


def states_body(plan):
    spans, heads, part, n = plan.spans, plan.heads, plan.part, plan.state

    def kernel(feat, step, log, into, cum_out, *outs):
        rows = lax.broadcasted_iota(jnp.int32, (CH, CH), 0)
        cols = lax.broadcasted_iota(jnp.int32, (CH, CH), 1)
        lower = (rows >= cols).astype(F32).astype(BF16)
        rates, tots = [], []
        for k in range(spans):
            at = slice(k * CH, (k + 1) * CH)
            cum = sum(dot(lower, p) for p in pieces(log[at, :], 3))
            cum_out[at, :] = cum
            tots.append(cum[CH - 1 : CH])
            rates.append(jnp.exp(cum[CH - 1 : CH] - cum) * step[at, :])
        tot = jnp.concatenate(tots + [sum(tots)] * (8 - spans), axis=0)
        for g in range(plan.groups):
            prefix_out, packed = outs[2 * g], outs[2 * g + 1]
            lanes = slice(g * part, (g + 1) * part)
            matrix = spread_matrix(heads, part, g * plan.group_heads, plan.head_width)
            high, mid, low = pieces(tot, 3)
            tot_wide = dot(high, matrix) + dot(mid, matrix) + dot(low, matrix)
            state = None
            for k in range(spans):
                at = slice(k * CH, (k + 1) * CH)
                scaled = (spread(rates[k], matrix) * feat[at, lanes].astype(F32)).astype(BF16)
                fresh = dot_rows(into[at, :], scaled)
                state = fresh if state is None else jnp.exp(tot_wide[k : k + 1]) * state + fresh
                if k + 1 < spans:
                    prefix_out[k] = state.astype(BF16)
            packed[:n, :] = state.astype(BF16)
            packed[n:, :] = pack_tail(tot_wide[spans : spans + 1], part)

    return kernel


def weights_body(plan):
    spans, heads, part, n, pw = plan.spans, plan.heads, plan.part, plan.state, plan.head_width

    def kernel(feat, step, cum_ref, into, outof, skip, *refs):
        prefixes = refs[: plan.groups]
        flipped = refs[plan.groups]
        partials = refs[plan.groups + 1 :]
        rows = lax.broadcasted_iota(jnp.int32, (CH, CH), 0)
        cols = lax.broadcasted_iota(jnp.int32, (CH, CH), 1)
        causal = rows >= cols
        left = cols < pw
        zero = jnp.zeros((CH, CH), BF16)
        for k in range(spans):
            at = slice(k * CH, (k + 1) * CH)
            score = lax.dot_general(
                outof[at, :], into[at, :], (((1,), (1,)), ((), ())), preferred_element_type=F32
            )
            score = jnp.where(causal, score, 0.0)
            cum = cum_ref[at, :]
            both = jnp.concatenate(
                [cum, step[at, :], jnp.zeros((CH, CH - 2 * heads), F32)], axis=1
            )
            turned = both.T
            for g in range(plan.groups):
                base = g * part
                matrix = spread_matrix(heads, part, g * plan.group_heads, pw)
                skip_wide = spread(jnp.broadcast_to(skip[...], (8, heads)), matrix)[0:1]
                rest = skip_wide * feat[at, base : base + part].astype(F32)
                if k > 0:
                    rest += spread(jnp.exp(cum), matrix) * dot(outof[at, :], prefixes[g][k - 1])
                for pair in range(plan.group_heads // 2):
                    lanes = slice(pair * 2 * pw, (pair + 1) * 2 * pw)
                    ws = []
                    for h in (0, 1):
                        head = g * plan.group_heads + 2 * pair + h
                        gap = cum[:, head : head + 1] - turned[head : head + 1, :]
                        decay = jnp.exp(jnp.minimum(gap, 0.0))
                        w = score * decay * turned[heads + head : heads + head + 1, :]
                        w = w.astype(BF16)
                        ws.append(w)
                        where = (g * plan.group_heads // 2 + pair) * 2 * CH
                        flipped[at, where + h * CH : where + (h + 1) * CH] = w.T
                    x = feat[at, base + pair * 2 * pw : base + (pair + 1) * 2 * pw]
                    stacked = jnp.concatenate(
                        [jnp.where(left, x, zero), jnp.where(left, zero, x)], axis=0
                    )
                    inside = dot(jnp.concatenate(ws, axis=1), stacked)
                    partials[g][at, lanes] = inside + rest[:, lanes]

    return kernel


def device_cum(cum_ref, spans):
    out, before = [], None
    for k in range(spans):
        cum = cum_ref[k * CH : (k + 1) * CH, :]
        out.append(cum if before is None else cum + before)
        before = out[-1][CH - 1 : CH]
    return jnp.concatenate(out, axis=0), before


def graph_body(plan, sides):
    tok = plan.tok

    def kernel(edges, counts, kern, cot, fwd_own, *refs):
        fwd_side, back_side = refs[:sides], refs[sides : 2 * sides]
        own_back = refs[2 * sides : 2 * sides + plan.groups]
        back_own = refs[2 * sides + plan.groups]
        bands = lax.axis_size("eta")
        band = lax.axis_index("eta")
        for ref in (fwd_own, back_own, *fwd_side, *back_side):
            ref[...] = jnp.zeros_like(ref)

        def spot(a, b):
            return (
                pl.ds(pl.multiple_of(a * BLOCK, BLOCK), BLOCK),
                pl.ds(pl.multiple_of(b * BLOCK, BLOCK), BLOCK),
            )

        if sides == 1:
            offsets, others = [2 - 2 * band], [1 - band]
        else:
            offsets, others = [0, 2][:sides], [band - 1, band + 1][:sides]

        def own(e, carry):
            off, src, dst, kind = (edges[band, 0, e, f] for f in range(4))
            tile = kern[kind]

            @pl.when(off == 1)
            def _():
                fwd_own[spot(dst, src)] = tile
                back_own[spot(src, dst)] = tile.T

            for s in range(sides):

                @pl.when(off == offsets[s])
                def _():
                    fwd_side[s][spot(dst, src)] = tile

            return carry

        lax.fori_loop(0, counts[band, 0], own, 0)
        for s in range(sides):
            real = (others[s] >= 0) & (others[s] < bands)
            other = jnp.clip(others[s], 0, bands - 1)

            def far(e, carry):
                off, src, dst, kind = (edges[other, 0, e, f] for f in range(4))

                @pl.when(off == 2 - offsets[s])
                def _():
                    back_side[s][spot(src, dst)] = kern[kind].T

                return carry

            lax.fori_loop(0, jnp.where(real, counts[other, 0], 0), far, 0)
        for g in range(plan.groups):
            lanes = slice(g * plan.part, (g + 1) * plan.part)
            own_back[g][...] = dot(back_own[...], cot[:, lanes]) + cot[:, lanes].astype(F32)

    return kernel


def grad_body(plan, sides, g):
    spans, heads, part, n = plan.spans, plan.heads, plan.part, plan.state

    def kernel(own_back, cum_ref, outof, *refs):
        mats, cots = refs[:sides], refs[sides : 2 * sides]
        grad, leaves, packed = refs[2 * sides :]
        matrix = spread_matrix(heads, part, g * plan.group_heads, plan.head_width)
        total = own_back[...]
        for s in range(sides):
            total += dot(mats[s][...], cots[s][...])
        rounded = total.astype(BF16)
        grad[...] = rounded
        tots = jnp.concatenate(
            [cum_ref[(k + 1) * CH - 1 : (k + 1) * CH, :] for k in range(spans)], axis=0
        )
        full = jnp.sum(tots, axis=0, keepdims=True)
        tots = jnp.concatenate([tots] + [full] * (8 - spans), axis=0)
        wide = sum(dot(p, matrix) for p in pieces(tots, 3))
        adjoint = None
        for k in reversed(range(spans)):
            at = slice(k * CH, (k + 1) * CH)
            scale = spread(jnp.exp(cum_ref[at, :]), matrix)
            fresh = dot_rows(outof[at, :], (scale * rounded[at].astype(F32)).astype(BF16))
            adjoint = fresh if adjoint is None else jnp.exp(wide[k : k + 1]) * adjoint + fresh
            if k > 0:
                leaves[k - 1] = adjoint.astype(BF16)
        packed[:n, :] = adjoint.astype(BF16)
        packed[n:, :] = pack_tail(wide[spans : spans + 1], part)

    return kernel


def grad_partial_body(plan, g):
    spans, heads, part, pw = plan.spans, plan.heads, plan.part, plan.head_width

    def kernel(flipped, grad, leaves, into, cum_ref, step, skip, partial):
        cols = lax.broadcasted_iota(jnp.int32, (CH, CH), 1)
        left = cols < pw
        zero = jnp.zeros((CH, CH), BF16)
        matrix = spread_matrix(heads, part, g * plan.group_heads, pw)
        skip_wide = spread(jnp.broadcast_to(skip[...], (8, heads)), matrix)[0:1]
        for k in range(spans):
            at = slice(k * CH, (k + 1) * CH)
            cum = cum_ref[at, :]
            rest = skip_wide * grad[at, :].astype(F32)
            if k + 1 < spans:
                rate = jnp.exp(cum[CH - 1 : CH] - cum) * step[at, :]
                rest += spread(rate, matrix) * dot(into[at, :], leaves[k])
            for pair in range(plan.group_heads // 2):
                lanes = slice(pair * 2 * pw, (pair + 1) * 2 * pw)
                where = (g * plan.group_heads // 2 + pair) * 2 * CH
                x = grad[at, lanes]
                stacked = jnp.concatenate(
                    [jnp.where(left, x, zero), jnp.where(left, zero, x)], axis=0
                )
                partial[at, lanes] = (
                    dot(flipped[at, where : where + 2 * CH], stacked) + rest[:, lanes]
                )

    return kernel


def merge_body(plan, bit, first, last, reverse):
    n = plan.state

    def kernel(own, got, *refs):
        if first:
            outs = refs
        else:
            enter_in, decay_in = refs[:2]
            outs = refs[2:]
        enter_out, decay_out, packed = outs
        here = lax.axis_index("seq")
        high = ((here >> bit) & 1) == 1
        before = high != reverse
        flag = jnp.where(before, 1.0, 0.0)
        log_own, log_got = unpack_tail(own, n), unpack_tail(got, n)
        s_own, s_got = own[:n, :].astype(F32), got[:n, :].astype(F32)
        if first:
            enter_out[...] = flag * s_got
            decay_out[...] = flag * jnp.broadcast_to(log_got, decay_out.shape)
        else:
            scale = flag * jnp.exp(decay_in[0:1, :])
            enter_out[...] = enter_in[...] + scale * s_got
            decay_out[...] = decay_in[...] + flag * log_got
        pass_own = jnp.where(before, 1.0, jnp.exp(log_got))
        pass_got = jnp.where(before, jnp.exp(log_own), 1.0)
        packed[:n, :] = (pass_own * s_own + pass_got * s_got).astype(BF16)
        packed[n:, :] = pack_tail(log_own + log_got, plan.part)

    return kernel


def last_body(plan, g, bit, first, reverse):
    spans, heads, part, n = plan.spans, plan.heads, plan.part, plan.state

    def kernel(got, *refs):
        if first:
            rest = refs
        else:
            enter_in, decay_in = refs[:2]
            rest = refs[2:]
        if reverse:
            partial, proj, cum_ref, step, out = rest[0], rest[1], rest[2], rest[3], rest[-1]
        else:
            partial, proj, cum_ref, out = rest
        here = lax.axis_index("seq")
        high = ((here >> bit) & 1) == 1
        flag = jnp.where(high != reverse, 1.0, 0.0)
        s_got = got[:n, :].astype(F32)
        if first:
            enter = flag * s_got
        else:
            enter = enter_in[...] + flag * jnp.exp(decay_in[0:1, :]) * s_got
        high_part, low_part = pieces(enter, 2)
        matrix = spread_matrix(heads, part, g * plan.group_heads, plan.head_width)
        cum, total = device_cum(cum_ref, spans)
        if reverse:
            scale = jnp.exp(total - cum) * step[...]
        else:
            scale = jnp.exp(cum)
        through = dot(proj[...], high_part) + dot(proj[...], low_part)
        out[...] = (partial[...] + spread(scale, matrix) * through).astype(BF16)

    return kernel


def message_body(plan):
    def kernel(mat, ssd, out):
        out[...] = dot(mat[...], ssd[...]) + ssd[...].astype(F32)

    return kernel


def layer_body(plan, sides):
    def kernel(own, *refs):
        mats, parts, out = refs[:sides], refs[sides : 2 * sides], refs[-1]
        total = own[...]
        for s in range(sides):
            total += dot(mats[s][...], parts[s][...])
        out[...] = total.astype(BF16)

    return kernel


def shards(
    features,
    step_sizes,
    log_decay,
    state_in,
    state_out,
    skip_gain,
    kernels,
    edge_lists,
    edge_counts,
    cotangent,
):
    _, tok, width = features.shape
    heads = step_sizes.shape[2]
    n = state_in.shape[2]
    plan = Plan(tok, width, heads, n)
    part, groups, spans = plan.part, plan.groups, plan.spans
    bands = lax.axis_size("eta")
    segs = lax.axis_size("seq")
    rounds = segs.bit_length() - 1
    assert segs == 1 << rounds and rounds > 0
    feat, step, log = features[0], step_sizes[0], log_decay[0]
    into, outof, cot = state_in[0], state_out[0], cotangent[0]
    skip = skip_gain[None, :]

    if bands == 2:
        routes = [[(0, 1), (1, 0)]]
    elif bands > 2:
        routes = [
            [(i, (i + 1) % bands) for i in range(bands)],
            [(i, (i - 1) % bands) for i in range(bands)],
        ]
    else:
        routes = []
    sides = len(routes)

    def across(x, name):
        out = []
        for s, route in enumerate(routes):
            with jax.named_scope(f"{name}_{s}"):
                out.append(lax.ppermute(x, "eta", route))
        return out

    def swap(x, bit, name):
        with jax.named_scope(name):
            return lax.ppermute(x, "seq", [(i, i ^ (1 << bit)) for i in range(segs)])

    lanes = [slice(g * part, (g + 1) * part) for g in range(groups)]
    cot_far = [across(cot[:, lanes[g]], f"xcot{g}") for g in range(groups)]

    res = run(
        states_body(plan),
        [shape((tok, heads), F32)]
        + [shape((spans - 1, n, part), BF16), shape((n + PAD, part), BF16)] * groups,
        (feat, step, log, into),
        us=4,
        name="states",
    )
    cum, prefixes, packs = res[0], res[1::2], res[2::2]

    def scan_rounds(packed, tag, reverse, g):
        carry = ()
        for bit in range(rounds):
            got = swap(packed, bit, f"z{tag}{g}r{bit}")
            if bit == rounds - 1:
                return got, carry
            enter, decay, packed = run(
                merge_body(plan, bit, bit == 0, False, reverse),
                [shape((n, part), F32), shape((8, part), F32), shape((n + PAD, part), BF16)],
                (packed, got, *carry),
                name=f"merge_{tag}{g}",
            )
            carry = (enter, decay)

    ready = [scan_rounds(packs[g], "f", False, g) for g in range(groups)]

    smem = pl.BlockSpec(memory_space=pltpu.SMEM)
    vmem = pl.BlockSpec(memory_space=pltpu.VMEM)
    square = shape((tok, tok), BF16)
    res = run(
        graph_body(plan, sides),
        [square] * (1 + 2 * sides) + [shape((tok, part), F32)] * groups,
        (edge_lists, edge_counts, kernels, cot),
        in_specs=[smem, smem, vmem, vmem],
        scratch_shapes=[pltpu.VMEM((tok, tok), BF16)],
        us=4,
        name="graph",
    )
    fwd_own, fwd_side, back_side = res[0], res[1 : 1 + sides], res[1 + sides : 1 + 2 * sides]
    own_back = res[1 + 2 * sides :]

    res = run(
        weights_body(plan),
        [shape((tok, heads * CH), BF16)] + [shape((tok, part), F32)] * groups,
        (feat, step, cum, into, outof, skip, *prefixes),
        us=8,
        name="weights",
    )
    flipped, partials = res[0], res[1:]

    grads, leaves, back_ready = [], [], []
    for g in range(groups):
        grad, leave, packed = run(
            grad_body(plan, sides, g),
            [shape((tok, part), BF16), shape((spans - 1, n, part), BF16), shape((n + PAD, part), BF16)],
            (own_back[g], cum, outof, *back_side, *cot_far[g]),
            us=3,
            name=f"grad{g}",
        )
        grads.append(grad)
        leaves.append(leave)
        back_ready.append(scan_rounds(packed, "b", True, g))

    ssds, ssd_far = [], []
    for g in range(groups):
        got, carry = ready[g]
        ssd = run(
            last_body(plan, g, rounds - 1, rounds == 1, False),
            shape((tok, part), BF16),
            (got, *carry, partials[g], outof, cum),
            us=2,
            name=f"ssd{g}",
        )
        ssds.append(ssd)
        ssd_far.append(across(ssd, f"xssd{g}"))

    owns = [
        run(message_body(plan), shape((tok, part), F32), (fwd_own, ssds[g]), us=2, name=f"own{g}")
        for g in range(groups)
    ]

    def placed(kernel, args, g, held, us, name):
        full = lambda a: pl.BlockSpec(a.shape, lambda i, nd=a.ndim: (0,) * nd)
        specs = [full(a) for a in args]
        aliases = {}
        if held is not None:
            aliases = {len(args): 0}
            args = (*args, held)
            specs.append(pl.BlockSpec(memory_space=pl.ANY))
        return run(
            kernel,
            shape((tok, width), BF16),
            args,
            in_specs=specs,
            out_specs=pl.BlockSpec((tok, part), lambda i, g=g: (0, g)),
            aliases=aliases,
            us=us,
            name=name,
            grid=(1,),
        )

    grad_out = None
    for g in range(groups):
        grad_partial = run(
            grad_partial_body(plan, g),
            shape((tok, part), F32),
            (flipped, grads[g], leaves[g], into, cum, step, skip),
            us=3,
            name=f"gradp{g}",
        )
        got, carry = back_ready[g]
        grad_out = placed(
            last_body(plan, g, rounds - 1, rounds == 1, True),
            (got, *carry, grad_partial, into, cum, step),
            g,
            grad_out,
            2,
            f"gradf{g}",
        )

    layer_out = None
    for g in range(groups):
        layer_out = placed(
            layer_body(plan, sides), (owns[g], *fwd_side, *ssd_far[g]), g, layer_out, 2, f"layer{g}"
        )

    return layer_out[None], grad_out[None]


def solution(mesh):
    return jax.shard_map(
        shards,
        mesh=mesh,
        in_specs=(
            P(("groups", "eta"), "seq", "rep"),
            P(("groups", "eta"), "seq", "rep"),
            P(("groups", "eta"), "seq", "rep"),
            P(("groups", "eta"), "seq", None),
            P(("groups", "eta"), "seq", None),
            P("rep"),
            P(),
            P("groups", "seq", None, None),
            P("groups", "seq"),
            P(("groups", "eta"), "seq", "rep"),
        ),
        out_specs=(P(("groups", "eta"), "seq", "rep"), P(("groups", "eta"), "seq", "rep")),
        check_vma=False,
    )
```

time: 172 us -> 99.7 us (0.58)
  Pallas kernels: 0 us -> 61.6 us
  matrix products: 44.4 us -> 0 us
  other arithmetic: 28.6 us -> 0 us
  local copies, waits for them, and re-layouts: 38.2 us -> 13.2 us
  between operations: 15 us -> 0.69 us
  blocking collectives: 11.4 us -> 0 us
  waiting for transfers between devices: 16.7 us -> 6.48 us
    pallas_call x0 -> x19, Pallas kernels: none -> 61.6 us  [run(): pl.pallas_call(kernel, out_shape=outs, in_specs=in_specs or [vmem] * len(...]
    dot_general x33 -> x0, matrix products: 44.4 us -> none  [the longest x4 6.97 us: span_forward(): jnp.einsum('in,hpn->ihp', out_span.astype(jnp.float32), state_now, precis...]
    all_gather x1 -> x0, blocking collectives: 11.4 us -> none  [entering_2(): everything = jax.tree.map(lambda part: lax.all_gather(part, axis), x)]
    ppermute x4 -> x12, waiting for transfers between devices: 16.6 us -> 6.48 us  [the longest x8 6.47 us: swap(): return lax.ppermute(x, 'seq', [(i, i ^ 1 << bit) for i in range(segs)])]
    convert_element_type x8 -> x0, other arithmetic: 10 us -> none  [the longest x1 3.81 us: shards(): ssd_grad = grad_rows.astype(jnp.bfloat16)]
    reshape x7 -> x0, local copies, waits for them, and re-layouts: 9.67 us -> none  [the longest x4 5.17 us: shards(): span_outputs.append(output.reshape(CH, feat_width))]
    select_n x8 -> x0, other arithmetic: 9.41 us -> none  [lap(): return jax.tree.map(lambda a, b: jnp.where(reached, a, b), new, before)]
    slice x10 -> x1, local copies, waits for them, and re-layouts: 6.12 us -> 0.07 us  [shards(): cot_far = [across(cot[:, lanes[g]], f'xcot{g}') for g in range(groups)]]
  transfers between devices with their start and end apart: 6 -> 12, of which waited for: 3 -> 2; matrix products, arithmetic and copies ran while one was open for 49% -> 1% of each run, Pallas kernels for 0% -> 55%
where the time goes in v1:
time: 99.7 us; the launch traced here: 98.8 us
  Pallas kernels  61.6 us (62%)
  starting transfers between devices  16.8 us (17%)
  local copies, waits for them, and re-layouts  13.2 us (13%)
  waiting for transfers between devices  6.48 us (6%)
    pallas_call x19, Pallas kernels, run(): pl.pallas_call(kernel, out_shape=outs, in_specs=in_specs or [vmem] * len(...  61.6 us
    unnamed x34, local copies, waits for them, and re-layouts  13.1 us
    ppermute x8, starting transfers between devices, swap(): return lax.ppermute(x, 'seq', [(i, i ^ 1 << bit) for i in range(segs)])  12.7 us
    ppermute x8, waiting for transfers between devices, swap(): return lax.ppermute(x, 'seq', [(i, i ^ 1 << bit) for i in range(segs)])  6.47 us
    ppermute x4, starting transfers between devices, across(): out.append(lax.ppermute(x, 'eta', route))  4.12 us
  transfers between devices with their start and end apart: 12, of which 2 were waited for; matrix products, arithmetic and copies ran while one was open for 1% of the time, Pallas kernels for 55%

profile of v1, /device:TPU:0, one launch (start us, length us, event | category | flops | bytes accessed | tf_op | source)
XLA Modules:
  0.0 98.8 jit_solution(14931099841519243317)
XLA Ops:
  0.6 1.7 %copy.16 = f32[1,512,16]{2,1,0:T(8,128)} copy(f32[1,512,16]{1,2,0:T(8,128)} %param.11) | data formatting | bytes 65536 | tf_op args[1]
  2.3 1.6 %copy.17 = f32[1,512,16]{2,1,0:T(8,128)} copy(f32[1,512,16]{1,2,0:T(8,128)} %param.12) | data formatting | bytes 65536 | tf_op args[2]
  3.9 4.3 %states.1 = (f32[512,16]{1,0:T(8,128)}, bf16[3,128,512]{2,1,0:T(8,128)(2,1)}, bf16[144,512]{1,0:T(8,128)(2,1)}, bf16[3,128,512]{2,1,0:T(8,128)(2,1)}, bf16[144,512]{1,0:T(8,128)(2,1)}) custom-call(bf16[512,1024]{1,0:T(8,128)(2,1)} %bitcast.25, f32[512,16]{1,0:T(8,128)} %bitcast.9, f32[512,16]{1,0:T(8,128)} %bitcast.32, bf16[512,128]{1,0:T(8,128)(2,1)} %bitcast.15), custom_call_target="tpu_custom_call" | custom-call | bytes 12000000 | tf_op jit(solution)/shard_map/states/pallas_call | solution.py:48
  8.3 3.0 %collective-permute-start = (bf16[144,512]{1,0:T(8,128)(2,1)}, bf16[144,512]{1,0:T(8,128)(2,1)S(1)}, u32[]{:S(2)}, u32[]{:S(2)}) collective-permute-start(bf16[144,512]{1,0:T(8,128)(2,1)} %get-tuple-element.34.own), channel_id=1, source_target_pairs={{0,4},{4,0},{8,12},{12,8},{1,5},{5,1},{9,13},{13,9},{2,6},{6,2},{1... | collective-permute-start | bytes 442376 | tf_op jit(solution)/shard_map/zf1r0/ppermute | solution.py:435
  11.3 0.1 fusion
  11.4 2.0 %collective-permute-start.9 = (bf16[512,512]{1,0:T(8,128)(2,1)S(1)}, bf16[512,512]{1,0:T(8,128)(2,1)S(1)}, u32[]{:S(2)}, u32[]{:S(2)}) collective-permute-start(bf16[512,512]{1,0:T(8,128)(2,1)S(1)} %get-tuple-element.64), channel_id=1, source_target_pairs={{0,2},{2,0},{1,3},{3,1},{4,6},{6,4},{5,7},{7,5},{8,10},{10,8},{9,1... | collective-permute-start | bytes 1572872 | tf_op jit(solution)/shard_map/xcot0_0/ppermute | solution.py:430
  13.4 0.1 collective-permute-start.6
  13.5 5.0 %collective-permute-done.3.got = bf16[144,512]{1,0:T(8,128)(2,1)S(1)} collective-permute-done((bf16[144,512]{1,0:T(8,128)(2,1)}, bf16[144,512]{1,0:T(8,128)(2,1)S(1)}, u32[]{:S(2)}, u32[]{:S(2)}) %collective-permute-start.3) | collective-permute-done | bytes 147488 | tf_op jit(solution)/shard_map/zf0r0/ppermute | solution.py:435
  18.5 0.7 copy-done.12
  19.2 1.8 %merge_f0.1 = (f32[128,512]{1,0:T(8,128)}, f32[8,512]{1,0:T(8,128)}, bf16[144,512]{1,0:T(8,128)(2,1)}) custom-call(bf16[144,512]{1,0:T(8,128)(2,1)} %get-tuple-element.43.own, bf16[144,512]{1,0:T(8,128)(2,1)} %copy-done.12), custom_call_target="tpu_custom_call" | custom-call | bytes 3000000 | tf_op jit(solution)/shard_map/merge_f0/pallas_call | solution.py:48
  21.0 2.8 %collective-permute-start.4 = (bf16[144,512]{1,0:T(8,128)(2,1)}, bf16[144,512]{1,0:T(8,128)(2,1)S(1)}, u32[]{:S(2)}, u32[]{:S(2)}) collective-permute-start(bf16[144,512]{1,0:T(8,128)(2,1)} %get-tuple-element.44), channel_id=1, source_target_pairs={{0,8},{4,12},{8,0},{12,4},{1,9},{5,13},{9,1},{13,5},{2,10},{6,14},... | collective-permute-start | bytes 442376 | tf_op jit(solution)/shard_map/zf0r1/ppermute | solution.py:435
  23.7 0.7 copy-done.9
  24.4 1.8 %merge_f1.1 = (f32[128,512]{1,0:T(8,128)}, f32[8,512]{1,0:T(8,128)}, bf16[144,512]{1,0:T(8,128)(2,1)}) custom-call(bf16[144,512]{1,0:T(8,128)(2,1)} %get-tuple-element.34.own, bf16[144,512]{1,0:T(8,128)(2,1)} %copy-done.9), custom_call_target="tpu_custom_call" | custom-call | bytes 3000000 | tf_op jit(solution)/shard_map/merge_f1/pallas_call | solution.py:48
  26.2 0.2 collective-permute-start.1
  26.3 8.2 %weights.1 = (bf16[512,2048]{1,0:T(8,128)(2,1)}, f32[512,512]{1,0:T(8,128)}, f32[512,512]{1,0:T(8,128)}) custom-call(bf16[512,1024]{1,0:T(8,128)(2,1)} %bitcast.26, f32[512,16]{1,0:T(8,128)} %bitcast.10, f32[512,16]{1,0:T(8,128)} %get-tuple-element.38.cum_ref.refs_4_, bf16[512,128]{1,0:T(8,128)(2,1)} %bitcast.16, bf16[512,128]{1,0:T(8,128)(2,1)} %bitcast.27, ...), custom_call_target="tpu_custom_call" | custom-call | bytes 24000000 | tf_op jit(solution)/shard_map/weights/pallas_call | solution.py:48
  34.5 0.7 copy-done.8
  35.2 3.0 %ssd0.1.ssd = bf16[512,512]{1,0:T(8,128)(2,1)} custom-call(bf16[144,512]{1,0:T(8,128)(2,1)} %copy-done.8, f32[128,512]{1,0:T(8,128)} %get-tuple-element.45.refs_0_, f32[8,512]{1,0:T(8,128)} %get-tuple-element.46.refs_1_, f32[512,512]{1,0:T(8,128)} %get-tuple-element.47.refs_2_, bf16[512,128]{1,0:T(8,128)(2,1)} %bitcast.28, ...), custom_call_target="tpu_custom_call" | custom-call | bytes 6000000 | tf_op jit(solution)/shard_map/ssd0/pallas_call | solution.py:48
  38.2 1.7 %collective-permute-start.5 = (bf16[512,512]{1,0:T(8,128)(2,1)}, bf16[512,512]{1,0:T(8,128)(2,1)S(1)}, u32[]{:S(2)}, u32[]{:S(2)}) collective-permute-start(bf16[512,512]{1,0:T(8,128)(2,1)} %ssd0.1.ssd), channel_id=1, source_target_pairs={{0,2},{2,0},{1,3},{3,1},{4,6},{6,4},{5,7},{7,5},{8,10},{10,8},{9,1... | collective-permute-start | bytes 1572872 | tf_op jit(solution)/shard_map/xssd0_0/ppermute | solution.py:430
  39.8 0.7 copy-done.7
  40.5 3.0 %ssd1.1.ssd = bf16[512,512]{1,0:T(8,128)(2,1)} custom-call(bf16[144,512]{1,0:T(8,128)(2,1)} %copy-done.7, f32[128,512]{1,0:T(8,128)} %get-tuple-element.36.refs_0_, f32[8,512]{1,0:T(8,128)} %get-tuple-element.37.refs_1_, f32[512,512]{1,0:T(8,128)} %get-tuple-element.41.refs_2_, bf16[512,128]{1,0:T(8,128)(2,1)} %bitcast.29, ...), custom_call_target="tpu_custom_call" | custom-call | bytes 6000000 | tf_op jit(solution)/shard_map/ssd1/pallas_call | solution.py:48
  43.5 0.4 collective-permute-start.2
  43.9 0.7 copy.14.edges
  44.6 0.6 copy.15.counts
  45.2 4.3 %graph.1 = (bf16[512,512]{1,0:T(8,128)(2,1)}, bf16[512,512]{1,0:T(8,128)(2,1)}, bf16[512,512]{1,0:T(8,128)(2,1)}, f32[512,512]{1,0:T(8,128)}, f32[512,512]{1,0:T(8,128)}) custom-call(s32[2,1,16,4]{3,2,1,0:T(8,128)} %copy.14.edges, s32[2,1]{1,0:T(2,128)} %copy.15.counts, bf16[4,128,128]{2,1,0:T(8,128)(2,1)} %kern.1, bf16[512,1024]{1,0:T(8,128)(2,1)} %bitcast.21), custom_call_target="tpu_custom_call" | custom-call | bytes 12000000 | tf_op jit(solution)/shard_map/graph/pallas_call | solution.py:48
  49.5 0.8 copy-done.2
  50.3 3.7 %grad0.1 = (bf16[512,512]{1,0:T(8,128)(2,1)}, bf16[3,128,512]{2,1,0:T(8,128)(2,1)}, bf16[144,512]{1,0:T(8,128)(2,1)}) custom-call(f32[512,512]{1,0:T(8,128)} %get-tuple-element.57.own_back, f32[512,16]{1,0:T(8,128)} %get-tuple-element.38.cum_ref.refs_4_, bf16[512,128]{1,0:T(8,128)(2,1)} %bitcast.30, bf16[512,512]{1,0:T(8,128)(2,1)} %get-tuple-element.49.refs_0_, ...), custom_call_target="tpu_custom_call" | custom-call | bytes 9000000 | tf_op jit(solution)/shard_map/grad0/pallas_call | solution.py:48
  54.0 2.0 %collective-permute-start.10 = (bf16[144,512]{1,0:T(8,128)(2,1)}, bf16[144,512]{1,0:T(8,128)(2,1)S(1)}, u32[]{:S(2)}, u32[]{:S(2)}) collective-permute-start(bf16[144,512]{1,0:T(8,128)(2,1)} %get-tuple-element.58.own), channel_id=1, source_target_pairs={{0,4},{4,0},{8,12},{12,8},{1,5},{5,1},{9,13},{13,9},{2,6},{6,2},{1... | collective-permute-start | bytes 442376 | tf_op jit(solution)/shard_map/zb0r0/ppermute | solution.py:435
  56.0 0.8 copy-done.1
  56.8 3.7 %grad1.1 = (bf16[512,512]{1,0:T(8,128)(2,1)}, bf16[3,128,512]{2,1,0:T(8,128)(2,1)}, bf16[144,512]{1,0:T(8,128)(2,1)}) custom-call(f32[512,512]{1,0:T(8,128)} %get-tuple-element.48.own_back, f32[512,16]{1,0:T(8,128)} %get-tuple-element.38.cum_ref.refs_4_, bf16[512,128]{1,0:T(8,128)(2,1)} %bitcast.31, bf16[512,512]{1,0:T(8,128)(2,1)} %get-tuple-element.49.refs_0_, ...), custom_call_target="tpu_custom_call" | custom-call | bytes 9000000 | tf_op jit(solution)/shard_map/grad1/pallas_call | solution.py:48
  60.5 0.7 copy-done.10
  61.2 1.8 %merge_b0.1 = (f32[128,512]{1,0:T(8,128)}, f32[8,512]{1,0:T(8,128)}, bf16[144,512]{1,0:T(8,128)(2,1)}) custom-call(bf16[144,512]{1,0:T(8,128)(2,1)} %get-tuple-element.58.own, bf16[144,512]{1,0:T(8,128)(2,1)} %copy-done.10), custom_call_target="tpu_custom_call" | custom-call | bytes 3000000 | tf_op jit(solution)/shard_map/merge_b0/pallas_call | solution.py:48
  63.0 3.0 %collective-permute-start.11 = (bf16[144,512]{1,0:T(8,128)(2,1)}, bf16[144,512]{1,0:T(8,128)(2,1)S(1)}, u32[]{:S(2)}, u32[]{:S(2)}) collective-permute-start(bf16[144,512]{1,0:T(8,128)(2,1)} %get-tuple-element.59), channel_id=1, source_target_pairs={{0,8},{4,12},{8,0},{12,4},{1,9},{5,13},{9,1},{13,5},{2,10},{6,14},... | collective-permute-start | bytes 442376 | tf_op jit(solution)/shard_map/zb0r1/ppermute | solution.py:435
  66.0 1.4 %collective-permute-done.7.got = bf16[144,512]{1,0:T(8,128)(2,1)S(1)} collective-permute-done((bf16[144,512]{1,0:T(8,128)(2,1)}, bf16[144,512]{1,0:T(8,128)(2,1)S(1)}, u32[]{:S(2)}, u32[]{:S(2)}) %collective-permute-start.7) | collective-permute-done | bytes 147488 | tf_op jit(solution)/shard_map/zb1r0/ppermute | solution.py:435
  67.4 0.7 copy-done.11
  68.1 1.8 %merge_b1.1 = (f32[128,512]{1,0:T(8,128)}, f32[8,512]{1,0:T(8,128)}, bf16[144,512]{1,0:T(8,128)(2,1)}) custom-call(bf16[144,512]{1,0:T(8,128)(2,1)} %get-tuple-element.50.own, bf16[144,512]{1,0:T(8,128)(2,1)} %copy-done.11), custom_call_target="tpu_custom_call" | custom-call | bytes 3000000 | tf_op jit(solution)/shard_map/merge_b1/pallas_call | solution.py:48
  69.9 1.7 %collective-permute-start.8 = (bf16[144,512]{1,0:T(8,128)(2,1)}, bf16[144,512]{1,0:T(8,128)(2,1)S(1)}, u32[]{:S(2)}, u32[]{:S(2)}) collective-permute-start(bf16[144,512]{1,0:T(8,128)(2,1)} %get-tuple-element.51), channel_id=1, source_target_pairs={{0,8},{4,12},{8,0},{12,4},{1,9},{5,13},{9,1},{13,5},{2,10},{6,14},... | collective-permute-start | bytes 442376 | tf_op jit(solution)/shard_map/zb1r1/ppermute | solution.py:435
  71.6 2.6 %own1.1.own = f32[512,512]{1,0:T(8,128)} custom-call(bf16[512,512]{1,0:T(8,128)(2,1)} %get-tuple-element.33.mat, bf16[512,512]{1,0:T(8,128)(2,1)} %ssd1.1.ssd), custom_call_target="tpu_custom_call" | custom-call | bytes 6000000 | tf_op jit(solution)/shard_map/own1/pallas_call | solution.py:48
  74.2 2.7 %own0.1.own = f32[512,512]{1,0:T(8,128)} custom-call(bf16[512,512]{1,0:T(8,128)(2,1)} %get-tuple-element.33.mat, bf16[512,512]{1,0:T(8,128)(2,1)} %ssd0.1.ssd), custom_call_target="tpu_custom_call" | custom-call | bytes 6000000 | tf_op jit(solution)/shard_map/own0/pallas_call | solution.py:48
  76.9 3.7 %gradp1.1.refs_2_ = f32[512,512]{1,0:T(8,128)} custom-call(bf16[512,2048]{1,0:T(8,128)(2,1)} %get-tuple-element.54.flipped, bf16[512,512]{1,0:T(8,128)(2,1)} %get-tuple-element.55.grad, bf16[3,128,512]{2,1,0:T(8,128)(2,1)} %get-tuple-element.56.leaves, bf16[512,128]{1,0:T(8,128)(2,1)} %bitcast.17, f32[512,16]{1,0:T(8,128)} %get-tuple-element.38.cum_ref.refs_4_, ...), custom_call_target="tpu_custom_call" | custom-call | bytes 9000000 | tf_op jit(solution)/shard_map/gradp1/pallas_call | solution.py:48
  80.6 3.7 %gradp0.1.refs_2_ = f32[512,512]{1,0:T(8,128)} custom-call(bf16[512,2048]{1,0:T(8,128)(2,1)} %get-tuple-element.54.flipped, bf16[512,512]{1,0:T(8,128)(2,1)} %get-tuple-element.62.grad, bf16[3,128,512]{2,1,0:T(8,128)(2,1)} %get-tuple-element.63.leaves, bf16[512,128]{1,0:T(8,128)(2,1)} %bitcast.18, f32[512,16]{1,0:T(8,128)} %get-tuple-element.38.cum_ref.refs_4_, ...), custom_call_target="tpu_custom_call" | custom-call | bytes 9000000 | tf_op jit(solution)/shard_map/gradp0/pallas_call | solution.py:48
  84.2 0.8 copy-done.3
  85.0 2.7 %layer0.1.refs_2_ = bf16[512,1024]{1,0:T(8,128)(2,1)} custom-call(f32[512,512]{1,0:T(8,128)} %own0.1.own, bf16[512,512]{1,0:T(8,128)(2,1)} %get-tuple-element.42.refs_0_, bf16[512,512]{1,0:T(8,128)(2,1)} %copy-done.3), custom_call_target="tpu_custom_call" | custom-call | bytes 6000000 | tf_op jit(solution)/shard_map/layer0/pallas_call | solution.py:48
  87.8 0.8 copy-done.4
  88.6 2.7 %layer1.1 = bf16[512,1024]{1,0:T(8,128)(2,1)} custom-call(f32[512,512]{1,0:T(8,128)} %own1.1.own, bf16[512,512]{1,0:T(8,128)(2,1)} %get-tuple-element.42.refs_0_, bf16[512,512]{1,0:T(8,128)(2,1)} %copy-done.4, bf16[512,1024]{1,0:T(8,128)(2,1)} %layer0.1.refs_2_), custom_call_target="tpu_custom_call", output_to_operand_aliasing={{}: (3, {})} | custom-call | bytes 6000000 | tf_op jit(solution)/shard_map/layer1/pallas_call | solution.py:48
  91.3 0.7 copy-done.5
  92.0 3.1 %gradf0.1.refs_6_ = bf16[512,1024]{1,0:T(8,128)(2,1)} custom-call(bf16[144,512]{1,0:T(8,128)(2,1)} %copy-done.5, f32[128,512]{1,0:T(8,128)} %get-tuple-element.60.refs_0_, f32[8,512]{1,0:T(8,128)} %get-tuple-element.61.refs_1_, f32[512,512]{1,0:T(8,128)} %gradp0.1.refs_2_, bf16[512,128]{1,0:T(8,128)(2,1)} %bitcast.19, ...), custom_call_target="tpu_custom_call" | custom-call | bytes 6000000 | tf_op jit(solution)/shard_map/gradf0/pallas_call | solution.py:48
  95.0 0.7 copy-done.6
  95.7 3.1 %gradf1.1 = bf16[512,1024]{1,0:T(8,128)(2,1)} custom-call(bf16[144,512]{1,0:T(8,128)(2,1)} %copy-done.6, f32[128,512]{1,0:T(8,128)} %get-tuple-element.52.refs_0_, f32[8,512]{1,0:T(8,128)} %get-tuple-element.53.refs_1_, f32[512,512]{1,0:T(8,128)} %gradp1.1.refs_2_, bf16[512,128]{1,0:T(8,128)(2,1)} %bitcast.20, ...), custom_call_target="tpu_custom_call", output_to_operand_aliasing={{}: (7, {})} | custom-call | bytes 6000000 | tf_op jit(solution)/shard_map/gradf1/pallas_call | solution.py:48
  (30 shorter events, 0.1 us)
Async XLA Ops:
  0.6 10.7 %copy-start = (bf16[1,512,1024]{2,1,0:T(8,128)(2,1)S(1)}, bf16[1,512,1024]{2,1,0:T(8,128)(2,1)}, u32[]{:S(2)}) copy-start(bf16[1,512,1024]{2,1,0:T(8,128)(2,1)} %param.19) | copy-start | bytes 3145732
  8.3 15.5 %collective-permute-start = (bf16[144,512]{1,0:T(8,128)(2,1)}, bf16[144,512]{1,0:T(8,128)(2,1)S(1)}, u32[]{:S(2)}, u32[]{:S(2)}) collective-permute-start(bf16[144,512]{1,0:T(8,128)(2,1)} %get-tuple-element.34.own), channel_id=1, source_target_pairs={{0,4},{4,0},{8,12},{12,8},{1,5},{5,1},{9,13},{13,9},{2,6},{6,2},{1... | collective-permute-start | bytes 442376 | tf_op jit(solution)/shard_map/zf1r0/ppermute | solution.py:435
  11.3 7.2 %collective-permute-start.3 = (bf16[144,512]{1,0:T(8,128)(2,1)}, bf16[144,512]{1,0:T(8,128)(2,1)S(1)}, u32[]{:S(2)}, u32[]{:S(2)}) collective-permute-start(bf16[144,512]{1,0:T(8,128)(2,1)} %get-tuple-element.43.own), channel_id=1, source_target_pairs={{0,4},{4,0},{8,12},{12,8},{1,5},{5,1},{9,13},{13,9},{2,6},{6,2},{1... | collective-permute-start | bytes 442376 | tf_op jit(solution)/shard_map/zf0r0/ppermute | solution.py:435
  11.4 38.1 %collective-permute-start.9 = (bf16[512,512]{1,0:T(8,128)(2,1)S(1)}, bf16[512,512]{1,0:T(8,128)(2,1)S(1)}, u32[]{:S(2)}, u32[]{:S(2)}) collective-permute-start(bf16[512,512]{1,0:T(8,128)(2,1)S(1)} %get-tuple-element.64), channel_id=1, source_target_pairs={{0,2},{2,0},{1,3},{3,1},{4,6},{6,4},{5,7},{7,5},{8,10},{10,8},{9,1... | collective-permute-start | bytes 1572872 | tf_op jit(solution)/shard_map/xcot0_0/ppermute | solution.py:430
  13.4 42.6 %collective-permute-start.6 = (bf16[512,512]{1,0:T(8,128)(2,1)S(1)}, bf16[512,512]{1,0:T(8,128)(2,1)S(1)}, u32[]{:S(2)}, u32[]{:S(2)}) collective-permute-start(bf16[512,512]{1,0:T(8,128)(2,1)S(1)} %get-tuple-element.65), channel_id=1, source_target_pairs={{0,2},{2,0},{1,3},{3,1},{4,6},{6,4},{5,7},{7,5},{8,10},{10,8},{9,1... | collective-permute-start | bytes 1572872 | tf_op jit(solution)/shard_map/xcot1_0/ppermute | solution.py:430
  18.5 0.7 copy-start.12
  21.0 13.5 %collective-permute-start.4 = (bf16[144,512]{1,0:T(8,128)(2,1)}, bf16[144,512]{1,0:T(8,128)(2,1)S(1)}, u32[]{:S(2)}, u32[]{:S(2)}) collective-permute-start(bf16[144,512]{1,0:T(8,128)(2,1)} %get-tuple-element.44), channel_id=1, source_target_pairs={{0,8},{4,12},{8,0},{12,4},{1,9},{5,13},{9,1},{13,5},{2,10},{6,14},... | collective-permute-start | bytes 442376 | tf_op jit(solution)/shard_map/zf0r1/ppermute | solution.py:435
  23.7 0.7 copy-start.9
  26.2 13.7 %collective-permute-start.1 = (bf16[144,512]{1,0:T(8,128)(2,1)}, bf16[144,512]{1,0:T(8,128)(2,1)S(1)}, u32[]{:S(2)}, u32[]{:S(2)}) collective-permute-start(bf16[144,512]{1,0:T(8,128)(2,1)} %get-tuple-element.35), channel_id=1, source_target_pairs={{0,8},{4,12},{8,0},{12,4},{1,9},{5,13},{9,1},{13,5},{2,10},{6,14},... | collective-permute-start | bytes 442376 | tf_op jit(solution)/shard_map/zf1r1/ppermute | solution.py:435
  34.5 0.7 copy-start.8
  35.2 8.7 %copy-start.13 = (s32[2,1,16,4]{2,3,1,0:T(4,128)S(1)}, s32[2,1,16,4]{2,3,1,0:T(4,128)}, u32[]{:S(2)}) copy-start(s32[2,1,16,4]{2,3,1,0:T(4,128)} %param.17) | copy-start | bytes 1540
  35.2 9.4 %copy-start.14 = (s32[2,1]{0,1:T(1,128)S(1)}, s32[2,1]{0,1:T(1,128)}, u32[]{:S(2)}) copy-start(s32[2,1]{0,1:T(1,128)} %param.18) | copy-start | bytes 28
  38.2 46.1 %collective-permute-start.5 = (bf16[512,512]{1,0:T(8,128)(2,1)}, bf16[512,512]{1,0:T(8,128)(2,1)S(1)}, u32[]{:S(2)}, u32[]{:S(2)}) collective-permute-start(bf16[512,512]{1,0:T(8,128)(2,1)} %ssd0.1.ssd), channel_id=1, source_target_pairs={{0,2},{2,0},{1,3},{3,1},{4,6},{6,4},{5,7},{7,5},{8,10},{10,8},{9,1... | collective-permute-start | bytes 1572872 | tf_op jit(solution)/shard_map/xssd0_0/ppermute | solution.py:430
  39.8 0.7 copy-start.7
  43.5 44.3 %collective-permute-start.2 = (bf16[512,512]{1,0:T(8,128)(2,1)}, bf16[512,512]{1,0:T(8,128)(2,1)S(1)}, u32[]{:S(2)}, u32[]{:S(2)}) collective-permute-start(bf16[512,512]{1,0:T(8,128)(2,1)} %ssd1.1.ssd), channel_id=1, source_target_pairs={{0,2},{2,0},{1,3},{3,1},{4,6},{6,4},{5,7},{7,5},{8,10},{10,8},{9,1... | collective-permute-start | bytes 1572872 | tf_op jit(solution)/shard_map/xssd1_0/ppermute | solution.py:430
  49.5 0.8 copy-start.2
  54.0 6.5 %collective-permute-start.10 = (bf16[144,512]{1,0:T(8,128)(2,1)}, bf16[144,512]{1,0:T(8,128)(2,1)S(1)}, u32[]{:S(2)}, u32[]{:S(2)}) collective-permute-start(bf16[144,512]{1,0:T(8,128)(2,1)} %get-tuple-element.58.own), channel_id=1, source_target_pairs={{0,4},{4,0},{8,12},{12,8},{1,5},{5,1},{9,13},{13,9},{2,6},{6,2},{1... | collective-permute-start | bytes 442376 | tf_op jit(solution)/shard_map/zb0r0/ppermute | solution.py:435
  56.0 0.8 copy-start.1
  60.5 6.9 %collective-permute-start.7 = (bf16[144,512]{1,0:T(8,128)(2,1)}, bf16[144,512]{1,0:T(8,128)(2,1)S(1)}, u32[]{:S(2)}, u32[]{:S(2)}) collective-permute-start(bf16[144,512]{1,0:T(8,128)(2,1)} %get-tuple-element.50.own), channel_id=1, source_target_pairs={{0,4},{4,0},{8,12},{12,8},{1,5},{5,1},{9,13},{13,9},{2,6},{6,2},{1... | collective-permute-start | bytes 442376 | tf_op jit(solution)/shard_map/zb1r0/ppermute | solution.py:435
  60.5 0.7 copy-start.10
  63.0 28.3 %collective-permute-start.11 = (bf16[144,512]{1,0:T(8,128)(2,1)}, bf16[144,512]{1,0:T(8,128)(2,1)S(1)}, u32[]{:S(2)}, u32[]{:S(2)}) collective-permute-start(bf16[144,512]{1,0:T(8,128)(2,1)} %get-tuple-element.59), channel_id=1, source_target_pairs={{0,8},{4,12},{8,0},{12,4},{1,9},{5,13},{9,1},{13,5},{2,10},{6,14},... | collective-permute-start | bytes 442376 | tf_op jit(solution)/shard_map/zb0r1/ppermute | solution.py:435
  67.4 0.7 copy-start.11
  69.9 25.2 %collective-permute-start.8 = (bf16[144,512]{1,0:T(8,128)(2,1)}, bf16[144,512]{1,0:T(8,128)(2,1)S(1)}, u32[]{:S(2)}, u32[]{:S(2)}) collective-permute-start(bf16[144,512]{1,0:T(8,128)(2,1)} %get-tuple-element.51), channel_id=1, source_target_pairs={{0,8},{4,12},{8,0},{12,4},{1,9},{5,13},{9,1},{13,5},{2,10},{6,14},... | collective-permute-start | bytes 442376 | tf_op jit(solution)/shard_map/zb1r1/ppermute | solution.py:435
  84.2 0.8 copy-start.3
  87.8 0.8 copy-start.4
  91.3 0.7 copy-start.5
  95.0 0.7 copy-start.6
